TPU v7x, 512 devices: a whole 4x8x8 slice. The times are simulated.
512 devices in a mesh: dp: 64 (over z, y), group: 8 (over x, core).
Axes of the slice: x: 4, y: 8, z: 8, core: 2. Of those that a mesh axis runs over, the one named last changes fastest.
Arguments:
- rewards: float32 [8192, 4096], P(('dp', 'group')), may hold values from -6 to 6
- values: float32 [8192, 4096], P(('dp', 'group')), may hold values from -6 to 6
- horizon: float32 [8192], P(('dp', 'group')), may hold values from 16 to 32768
- lengths: int32 [8192], P(('dp', 'group')), may hold values from 1 to 4096
- assignment: int32 [64, 4096], P('dp', 'group'), may hold values from 0 to 4095, as said below
Outputs:
- returns: float32 [8192, 4096], P(('dp', 'group'))
- train_adv: float32 [262144, 128], P(('dp', 'group'))
Inputs may be any that keep to these rules, and one draw needn't show every extreme that they name: Each row of assignment names each of the 4096 blocks of its index of dp once; the slots held by one device take at most 128 blocks from the sequences of any one device of its group, and that most is reached in every row.
All inputs are finite; a program needn't handle non-finite values.
Results may differ from a plain program's by a relative error of at most 0.0001.
Values sent between devices are 32-bit elements; how exact they have to be, the bound alone decides.
A program may use at most 64 MiB of HBM per device.

v0:
```python
import jax
import jax.numpy as jnp
from jax import lax
from jax.sharding import PartitionSpec as P

LEN = 4096
BLK = 128


trace_decay = 0.998
epsilon = 1e-05


def copy_for_each(shard, axis):
    copies = jnp.broadcast_to(shard, (lax.axis_size(axis), *shard.shape))
    return lax.all_to_all(copies, axis, split_axis=0, concat_axis=0, tiled=True)


def all_in_one(shard, axis):
    leaves = jax.tree.leaves(shard)
    sequence = sorted(range(len(leaves)), key=lambda k: -leaves[k].size)
    width = (1, *leaves[sequence[0]].shape)[-1]
    lines = [
        jnp.pad(leaves[k].reshape(-1), (0, -leaves[k].size % width)).reshape(-1, width)
        for k in sequence
    ]
    both, at, found = (copy_for_each(jnp.concatenate(lines), axis), 0, {})
    for k, line in zip(sequence, lines):
        share = both[:, at : at + len(line)].reshape(len(both), -1)
        found[k] = share[:, : leaves[k].size].reshape(-1, *leaves[k].shape)
        at += len(line)
    numbers = iter(range(len(leaves)))
    return jax.tree.map(lambda _: found[next(numbers)], shard)


def combined_pairwise(pieces, combine):
    while len(jax.tree.leaves(pieces)[0]) > 1:
        pieces = jax.vmap(combine)(
            *(jax.tree.map(lambda part: part[side::2], pieces) for side in (0, 1))
        )
    return jax.tree.map(lambda part: part[0], pieces)


def combined_all(shard, axis, combine):
    pieces = all_in_one(shard, axis)
    return combined_pairwise(pieces, combine)


def once_a_type(shard, axis):
    leaves, found = (jax.tree.leaves(shard), {})
    for initial, a in enumerate(leaves):
        if initial not in found:
            alike = [k for k, b in enumerate(leaves) if b.dtype == a.dtype]
            got = (
                all_in_one([leaves[k] for k in alike], axis)
                if len(alike) > 1
                else [copy_for_each(a, axis)]
            )
            for k, b in zip(alike, got):
                found[k] = b
    numbers = iter(range(len(leaves)))
    return jax.tree.map(lambda _: found[next(numbers)], shard)


def combined_all_2(shard, axis, combine):
    pieces = once_a_type(shard, axis)
    return combined_pairwise(pieces, combine)


def laid_out(tiles, dim):
    shape = list(tiles.shape[1:])
    shape[dim] *= tiles.shape[0]
    return jnp.moveaxis(tiles, 0, dim).reshape(shape)


def gathered_copies(shard, axis, dim):
    tiles = copy_for_each(shard, axis)
    return laid_out(tiles, dim)


def merge_moments(first, second):
    total = first[0] + second[0]
    safe = jnp.maximum(total, 1.0)
    offset = second[1] - first[1]
    center = first[1] + offset * second[0] / safe
    spread = first[2] + second[2] + offset * offset * first[0] * second[0] / safe
    return (total, center, spread)


def blocked_discount(deltas, coeff, per_row, width):
    seqs = deltas.shape[0]
    log_rate = jnp.log(coeff)
    stacked = deltas.reshape(seqs, per_row, width)
    inner = jnp.arange(width, dtype=jnp.int32)
    gap = (inner[None, :] - inner[:, None]).astype(jnp.float32)
    within = jnp.where(
        gap[None, :, :] >= 0.0,
        jnp.exp(jnp.maximum(gap, 0.0)[None, :, :] * log_rate[:, None, None]),
        0.0,
    )
    partial_sums = jnp.einsum("sbj,sij->sbi", stacked, within, precision=lax.Precision.HIGHEST)
    block_sums = partial_sums[:, :, 0]
    outer = jnp.arange(per_row, dtype=jnp.int32)
    step_gap = (outer[None, :] - outer[:, None]).astype(jnp.float32)
    across = jnp.where(
        step_gap[None, :, :] >= 0.0,
        jnp.exp(jnp.maximum(step_gap, 0.0)[None, :, :] * (width * log_rate)[:, None, None]),
        0.0,
    )
    starts = jnp.einsum("sc,sbc->sb", block_sums, across, precision=lax.Precision.HIGHEST)
    following = jnp.concatenate([starts[:, 1:], jnp.zeros((seqs, 1), jnp.float32)], axis=1)
    tail_power = jnp.exp((width - inner).astype(jnp.float32)[None, :] * log_rate[:, None])
    total = partial_sums + following[:, :, None] * tail_power[:, None, :]
    return total.reshape(seqs, per_row * width)


def body(rewards, values, horizon, lengths, assignment):
    seqs, local = rewards.shape
    position = jnp.arange(local, dtype=jnp.int32)
    inside = position[None, :] < lengths[:, None]
    follows = position[None, :] + 1 < lengths[:, None]
    shifted = jnp.concatenate([values[:, 1:], jnp.zeros((seqs, 1), jnp.float32)], axis=1)
    upcoming = jnp.where(follows, shifted, 0.0)
    discount = 1.0 - 1.0 / horizon
    deltas = jnp.where(inside, rewards + discount[:, None] * upcoming - values, 0.0)
    per_row = LEN // BLK
    advantage = blocked_discount(deltas, discount * trace_decay, per_row, BLK)
    returns = jnp.where(inside, advantage + values, 0.0)
    weight = inside.astype(jnp.float32)
    counted = jnp.sum(weight)
    center = jnp.sum(advantage * weight) / jnp.maximum(counted, 1.0)
    spread = jnp.sum(weight * (advantage - center) ** 2)
    moments = (counted, center, spread)
    moments = combined_all(moments, "group", merge_moments)
    moments = combined_all_2(moments, "dp", merge_moments)
    total, middle, deviation = moments
    scale = lax.rsqrt(deviation / total + epsilon)
    slots = assignment.shape[-1]
    wanted = assignment.reshape(slots)
    empty = jnp.zeros((slots, BLK), jnp.float32)
    blocks = advantage.reshape(seqs, per_row, BLK)
    owner = wanted // per_row
    pieces = (gathered_copies(blocks, "group", 0), gathered_copies(lengths, "group", 0))
    piece = pieces[0]
    labels = (
        jnp.arange(piece.shape[0], dtype=jnp.int32)[:, None] * per_row
        + jnp.arange(per_row, dtype=jnp.int32)[None, :]
    )
    onehot = (wanted[:, None] == labels.reshape(1, -1)).astype(jnp.float32)
    flat = piece.reshape(piece.shape[0] * per_row, BLK)
    moved_part = jnp.dot(
        onehot, flat, precision=lax.Precision.HIGHEST, preferred_element_type=jnp.float32
    )
    ident = jnp.arange(pieces[1].shape[0], dtype=jnp.int32)
    found = jnp.sum(jnp.where(owner[:, None] == ident[None, :], pieces[1][None, :], 0), axis=1)
    limit = (empty, jnp.zeros((slots,), jnp.int32))[1] + found
    within = wanted % per_row
    spot = within[:, None] * BLK + jnp.arange(BLK, dtype=jnp.int32)[None, :]
    train = jnp.where(spot < limit[:, None], (moved_part - middle) * scale, 0.0)
    return (returns, train)


def solution(mesh):
    in_specs = (
        P(("dp", "group"), None),
        P(("dp", "group"), None),
        P(("dp", "group")),
        P(("dp", "group")),
        P("dp", "group"),
    )
    out_specs = (P(("dp", "group"), None), P(("dp", "group"), None))
    return jax.shard_map(body, mesh=mesh, in_specs=in_specs, out_specs=out_specs, check_vma=False)
```

profile of v0, /device:TPU:1, one launch (start us, length us, event | category | flops | bytes accessed | tf_op | source)
XLA Modules:
  0.0 103.3 jit_solution(12477975972292106711)
XLA Ops:
  0.8 0.7 broadcast_multiply_fusion
  1.4 1.1 %slice.201 = f32[16,4095]{1,0:T(8,128)S(1)} slice(f32[16,4096]{1,0:T(8,128)} %param.6), slice={[0:16], [1:4096]} | slice | bytes 524160 | tf_op jit(solution)/shard_map/slice | solution.py:122
  2.6 1.2 %select_bitcast_fusion = f32[2,8,32,128]{3,1,2,0:T(8,128)S(1)} fusion(f32[16,4096]{1,0:T(8,128)} %param.6, f32[16,4096]{1,0:T(8,128)} %param.5, f32[16,4095]{1,0:T(8,128)S(1)} %slice.201, s32[4096]{0:T(1024)S(1)} %iota_add_fusion.1, f32[16]{0:T(128)S(1)} %get-tuple-element.25, s32[16]{0:T(128)} %param.8), kind=kLoop, calls=%fused_computation.31 | loop fusion | flops 458752 | bytes 1065024
  3.8 1.8 %fusion.13 = f32[16,32,128]{2,1,0:T(8,128)S(1)} fusion(f32[16,32,128]{2,1,0:T(8,128)S(1)} %bitcast.32, f32[16]{0:T(128)S(1)} %multiply_log_fusion, f32[128,128]{1,0:T(8,128)S(1)} %convert_maximum_fusion, pred[128,128]{1,0:T(8,128)(4,1)S(1)} %convert_compare_fusion), kind=kOutput, calls=%fused_computation.7 | convolution fusion | flops 101187584 | bytes 606272 | tf_op jit(solution)/shard_map/sbj,sij->sbi/dot_general | solution.py:101
  5.7 0.1 slice_reduce_fusion
  5.8 0.6 fusion.24
  6.6 0.8 fusion.21
  7.3 1.6 %convert_reduce_fusion = (f32[]{:T(128)}, f32[16,4096]{1,0:T(8,128)}) fusion(s32[16]{0:T(128)S(1)} %copy-done.1, f32[16,4096]{1,0:T(8,128)S(1)} %copy-done, f32[2,8,32,128]{3,2,1,0:T(8,128)S(1)} %bitcast.30), kind=kLoop, calls=%fused_computation.22 | loop fusion | flops 327679 | bytes 786500 | tf_op jit(solution)/shard_map/reduce_sum | solution.py:130
  10.3 0.7 fusion.22
  11.0 1.3 %maximum_bitcast_fusion = f32[3]{0:T(128)S(1)} fusion(f32[1,1]{0,1:T(1,128)} %bitcast.7, f32[1,1]{0,1:T(1,128)} %bitcast.6, f32[1,1]{0,1:T(1,128)} %bitcast.5), kind=kLoop, calls=%fused_computation.62 | loop fusion | flops 6 | bytes 24 | tf_op jit(solution)/shard_map/concatenate | solution.py:27
  12.3 0.6 broadcast_in_dim.96
  12.9 10.1 %all-to-all-start.2 = ((f32[8,3,1]{1,2,0:T(1,128)}), f32[8,3,1]{1,2,0:T(1,128)S(1)}, u32[]{:S(2)}, u32[]{:S(2)}) async-start(f32[8,3,1]{1,2,0:T(1,128)} %broadcast_in_dim.96), calls=%async_computation.2 | async-start | bytes 8192 | tf_op jit(solution)/shard_map/all_to_all | solution.py:16
  23.2 4.4 %all-to-all-done.2 = f32[8,3,1]{1,2,0:T(1,128)S(1)} async-done(((f32[8,3,1]{1,2,0:T(1,128)}), f32[8,3,1]{1,2,0:T(1,128)S(1)}, u32[]{:S(2)}, u32[]{:S(2)}) %all-to-all-start.2) | async-done | bytes 128 | tf_op jit(solution)/shard_map/all_to_all | solution.py:16
  27.5 0.6 broadcast_in_dim.91
  28.1 3.9 %all-to-all-start = ((s32[8,1,16]{2,1,0:T(1,128)}), s32[8,1,16]{2,1,0:T(1,128)S(1)}, u32[]{:S(2)}, u32[]{:S(2)}) async-start(s32[8,1,16]{2,1,0:T(1,128)} %broadcast_in_dim.91), calls=%async_computation | async-start | bytes 8192 | tf_op jit(solution)/shard_map/all_to_all | solution.py:16
  32.0 0.2 slice_reduce_fusion.5
  32.2 0.1 slice.205
  33.4 0.7 fusion.39
  39.3 0.6 fusion.41
  41.2 0.6 broadcast_in_dim.97
  41.9 12.0 %all-to-all-start.3 = ((f32[64,3,1]{1,2,0:T(1,128)}), f32[64,3,1]{1,2,0:T(1,128)S(1)}, u32[]{:S(2)}, u32[]{:S(2)}) async-start(f32[64,3,1]{1,2,0:T(1,128)} %broadcast_in_dim.97), calls=%async_computation.3 | async-start | bytes 65536 | tf_op jit(solution)/shard_map/all_to_all | solution.py:16
  53.9 0.6 broadcast.244
  54.5 0.7 reduce.19
  55.3 0.2 select_reduce_fusion
  55.5 9.2 %all-to-all-done.3 = f32[64,3,1]{1,2,0:T(1,128)S(1)} async-done(((f32[64,3,1]{1,2,0:T(1,128)}), f32[64,3,1]{1,2,0:T(1,128)S(1)}, u32[]{:S(2)}, u32[]{:S(2)}) %all-to-all-start.3) | async-done | bytes 800 | tf_op jit(solution)/shard_map/all_to_all | solution.py:16
  64.7 1.6 %broadcast_in_dim.95 = f32[8,16,32,128]{3,2,1,0:T(8,128)} broadcast(f32[16,32,128]{2,1,0:T(8,128)S(1)} %get-tuple-element.23), dimensions={1,2,3} | broadcast | bytes 2359296 | tf_op jit(solution)/shard_map/broadcast_in_dim | solution.py:15
  66.3 6.2 %all-to-all-start.1 = ((f32[8,16,32,128]{3,2,1,0:T(8,128)}), f32[8,16,32,128]{3,2,1,0:T(8,128)S(1)}, u32[]{:S(2)}, u32[]{:S(2)}) async-start(f32[8,16,32,128]{3,2,1,0:T(8,128)} %broadcast_in_dim.95), calls=%async_computation.1 | async-start | bytes 4194304 | tf_op jit(solution)/shard_map/all_to_all | solution.py:16
  72.6 1.8 %slice_reduce_fusion.3 = (f32[64]{0:T(128)S(1)}, f32[64]{0:T(128)S(1)}, f32[64]{0:T(128)S(1)}) fusion(f32[64,3,1]{1,2,0:T(1,128)S(1)} %all-to-all-done.3), kind=kLoop, calls=%fused_computation.43 | loop fusion | bytes 1536 | tf_op jit(solution)/shard_map/slice | solution.py:29
  74.4 0.1 slice.226
  74.5 0.1 slice.227
  74.7 0.1 slice.229
  74.8 0.1 slice.230
  74.9 0.1 slice.231
  75.0 0.1 slice.232
  75.1 0.1 slice.233
  75.2 0.1 slice.234
  75.6 0.1 slice.237
  75.7 0.1 slice.238
  75.8 0.1 slice.239
  76.6 0.1 slice.252
  76.7 0.1 slice.253
  76.8 0.1 slice.254
  77.0 0.1 slice.255
  77.7 0.6 fusion.37
  79.6 0.6 fusion.36
  84.0 0.6 fusion.38
  85.9 12.8 %all-to-all-done.1 = f32[8,16,32,128]{3,2,1,0:T(8,128)S(1)} async-done(((f32[8,16,32,128]{3,2,1,0:T(8,128)}), f32[8,16,32,128]{3,2,1,0:T(8,128)S(1)}, u32[]{:S(2)}, u32[]{:S(2)}) %all-to-all-start.1) | async-done | bytes 2097184 | tf_op jit(solution)/shard_map/all_to_all | solution.py:16
  98.8 4.5 %fusion.10 = f32[512,128]{1,0:T(8,128)} fusion(f32[4096,128]{1,0:T(8,128)S(1)} %bitcast.31, s32[4096]{0:T(1024)S(1)} %add.204, s32[512]{0:T(512)S(1)} %bitcast.36, f32[]{:T(128)} %bitcast.14, f32[]{:T(128)} %bitcast.13, s32[512]{0:T(512)S(1)} %select_reduce_fusion, s32[512]{0:T(512)S(1)} %get-tuple-element.26), kind=kOutput, calls=%fused_computation.6 | convolution fusion | flops 3223650304 | bytes 2381832 | tf_op jit(solution)/shard_map/dot_general | solution.py:151
  (65 shorter events, 3.3 us)
Async XLA Ops:
  0.6 6.0 %copy-start.1 = (s32[16]{0:T(128)S(1)}, s32[16]{0:T(128)}, u32[]{:S(2)}) copy-start(s32[16]{0:T(128)} %param.8) | copy-start | bytes 196
  1.4 5.9 %copy-start = (f32[16,4096]{1,0:T(8,128)S(1)}, f32[16,4096]{1,0:T(8,128)}, u32[]{:S(2)}) copy-start(f32[16,4096]{1,0:T(8,128)} %param.6) | copy-start | bytes 786436
  3.8 19.2 %copy-start.2 = (s32[1,512]{1,0:T(1,128)S(1)}, s32[1,512]{1,0:T(1,128)}, u32[]{:S(2)}) copy-start(s32[1,512]{1,0:T(1,128)} %param.9) | copy-start | bytes 6148
  12.9 14.6 %all-to-all-start.2 = ((f32[8,3,1]{1,2,0:T(1,128)}), f32[8,3,1]{1,2,0:T(1,128)S(1)}, u32[]{:S(2)}, u32[]{:S(2)}) async-start(f32[8,3,1]{1,2,0:T(1,128)} %broadcast_in_dim.96), calls=%async_computation.2 | async-start | bytes 8192 | tf_op jit(solution)/shard_map/all_to_all | solution.py:16
  28.1 13.1 %all-to-all-start = ((s32[8,1,16]{2,1,0:T(1,128)}), s32[8,1,16]{2,1,0:T(1,128)S(1)}, u32[]{:S(2)}, u32[]{:S(2)}) async-start(s32[8,1,16]{2,1,0:T(1,128)} %broadcast_in_dim.91), calls=%async_computation | async-start | bytes 8192 | tf_op jit(solution)/shard_map/all_to_all | solution.py:16
  41.9 22.8 %all-to-all-start.3 = ((f32[64,3,1]{1,2,0:T(1,128)}), f32[64,3,1]{1,2,0:T(1,128)S(1)}, u32[]{:S(2)}, u32[]{:S(2)}) async-start(f32[64,3,1]{1,2,0:T(1,128)} %broadcast_in_dim.97), calls=%async_computation.3 | async-start | bytes 65536 | tf_op jit(solution)/shard_map/all_to_all | solution.py:16
  66.3 32.5 %all-to-all-start.1 = ((f32[8,16,32,128]{3,2,1,0:T(8,128)}), f32[8,16,32,128]{3,2,1,0:T(8,128)S(1)}, u32[]{:S(2)}, u32[]{:S(2)}) async-start(f32[8,16,32,128]{3,2,1,0:T(8,128)} %broadcast_in_dim.95), calls=%async_computation.1 | async-start | bytes 4194304 | tf_op jit(solution)/shard_map/all_to_all | solution.py:16
where the time goes:
time: 104 us; the launch traced here: 103 us
  starting transfers between devices  32.2 us (31%)
  waiting for transfers between devices  26.4 us (25%)
  between operations  15.1 us (15%)
  local copies, waits for them, and re-layouts  15 us (14%)
  other arithmetic  7.65 us (7%)
  matrix products  6.89 us (7%)
    all_to_all x4, starting transfers between devices, copy_for_each(): return lax.all_to_all(copies, axis, split_axis=0, concat_axis=0, tiled=True)  32.2 us
    all_to_all x4, waiting for transfers between devices, copy_for_each(): return lax.all_to_all(copies, axis, split_axis=0, concat_axis=0, tiled=True)  26.4 us
    slice x47, local copies, waits for them, and re-layouts, combined_pairwise(): part[side::2]  7.34 us
    dot_general x1, matrix products, body(): jnp.dot(onehot, flat, precision=lax.Precision.HIGHEST, preferred_element_...  4.48 us
    broadcast_in_dim x4, local copies, waits for them, and re-layouts, copy_for_each(): copies = jnp.broadcast_to(shard, (lax.axis_size(axis), *shard.shape))  3.45 us
  transfers between devices with their start and end apart: 4, of which 3 were waited for; matrix products, arithmetic and copies ran while one was open for 11% of the time, Pallas kernels for 0%

commit v1 on v0

v1 whole, which is shorter than its diff:
```python
import jax
import jax.numpy as jnp
from jax import lax
from jax.experimental import pallas as pl
from jax.experimental.pallas import tpu as pltpu
from jax.sharding import PartitionSpec as P

LEN = 4096
BLK = 128
SEQ = 16
NBLK = LEN // BLK
ROWS = SEQ * NBLK
HALF = ROWS // 2
TRACE_DECAY = 0.998
EPSILON = 1e-05
OUTSIDE = 1e30
LIMIT = 1e29
CHUNK = 8
MESH = pl.DeviceIdType.MESH


def column(row):
    wide = jnp.broadcast_to(row, (SEQ, SEQ))
    down = lax.broadcasted_iota(jnp.int32, (SEQ, SEQ), 0)
    across = lax.broadcasted_iota(jnp.int32, (SEQ, SEQ), 1)
    picked = jnp.sum(jnp.where(down == across, wide, 0.0), axis=1, keepdims=True)
    return jnp.broadcast_to(picked, (SEQ, BLK))


def merged(buf):
    n, m, s = buf[:, 0, :], buf[:, 1, :], buf[:, 2, :]
    total = jnp.sum(n, axis=0, keepdims=True)
    mean = jnp.sum(n * m, axis=0, keepdims=True) / total
    gap = m - mean
    spread = jnp.sum(s + n * gap * gap, axis=0, keepdims=True)
    return total, mean, spread


def kernel(rew_hbm, val_hbm, hor_hbm, len_hbm, asg_hbm, ret_hbm, train_hbm,
           rew, val, hor, lens, asg, ret, gath, rows, mom,
           in_sem, out_sem, mom_send, mom_recv, data_send, data_recv):
    d = lax.axis_index("dp")
    g = lax.axis_index("group")
    y, z = lax.rem(d, 8), d // 8
    group_peers = [(d, lax.rem(g + k, 8)) for k in range(1, 8)]
    y_peers = [(z * 8 + lax.rem(y + k, 8), g) for k in range(1, 8)]
    z_peers = [(lax.rem(d + 8 * k, 64), g) for k in range(1, 8)]

    barrier = pltpu.get_barrier_semaphore()
    for peer in z_peers + y_peers + group_peers:
        pl.semaphore_signal(barrier, inc=1, device_id=peer, device_id_type=MESH)

    loads = [
        pltpu.make_async_copy(src, dst, in_sem.at[i])
        for i, (src, dst) in enumerate(
            [(hor_hbm, hor), (len_hbm, lens), (val_hbm, val), (rew_hbm, rew), (asg_hbm, asg)])
    ]
    for load in loads:
        load.start()
    for load in loads[:4]:
        load.wait()

    lane = lax.broadcasted_iota(jnp.int32, (SEQ, BLK), 1)
    length = column(lens[...].astype(jnp.float32)).astype(jnp.int32)
    gamma = 1.0 - 1.0 / column(hor[...])
    powers = [gamma * TRACE_DECAY]
    for _ in range(7):
        powers.append(powers[-1] * powers[-1])
    steps = [jnp.where(lane < BLK - (1 << k), powers[k], 0.0) for k in range(7)]
    togo = BLK - lane
    tail = jnp.where(togo == BLK, powers[7], 1.0)
    for k in range(7):
        tail = tail * jnp.where(((togo >> k) & 1) == 1, powers[k], 1.0)

    zero = jnp.zeros((SEQ, BLK), jnp.float32)
    carry, ahead, total = zero, zero, zero
    shape = (CHUNK, SEQ, BLK)
    for first in range(NBLK - CHUNK, -1, -CHUNK):
        cols = [slice((first + i) * BLK, (first + i + 1) * BLK) for i in range(CHUNK)]
        v = jnp.stack([val[:, c] for c in cols])
        r = jnp.stack([rew[:, c] for c in cols])
        turned = pltpu.roll(v, BLK - 1, 2)
        following = jnp.concatenate([turned[1:], ahead[None]], axis=0)
        ahead = turned[0]
        shifted = jnp.where(lane[None] < BLK - 1, turned, following)
        block = lax.broadcasted_iota(jnp.int32, shape, 0) + first
        left = length[None] - block * BLK
        inside = lane[None] < left
        follows = lane[None] + 1 < left
        part = jnp.where(inside, r + gamma[None] * jnp.where(follows, shifted, 0.0) - v, 0.0)
        for k in range(7):
            part = part + steps[k][None] * pltpu.roll(part, BLK - (1 << k), 2)
        head = jnp.broadcast_to(part[:, :, 0:1], shape)
        for i in range(CHUNK - 1, -1, -1):
            adv = part[i] + tail * carry
            carry = head[i] + powers[7] * carry
            total = total + adv
            ret[:, cols[i]] = jnp.where(inside[i], adv + v[i], 0.0)
            sent = jnp.where(inside[i], adv, OUTSIDE)
            at = (first + i) * 8
            gath[g, at:at + 8, :] = sent[:8]
            gath[g, HALF + at:HALF + at + 8, :] = sent[8:]
    give_returns = pltpu.make_async_copy(ret, ret_hbm, out_sem.at[0])
    give_returns.start()

    count = jnp.sum(jnp.sum(length[:, 0:1].astype(jnp.float32), axis=0, keepdims=True), axis=1, keepdims=True)
    mean = jnp.sum(jnp.sum(total, axis=0, keepdims=True), axis=1, keepdims=True) / count
    square = jnp.zeros((8, BLK), jnp.float32)
    for i in range(ROWS // 64):
        own = gath[g, i * 64:(i + 1) * 64, :]
        gap = jnp.where(own < LIMIT, own - mean, 0.0)
        square = square + jnp.sum((gap * gap).reshape(8, 8, BLK), axis=0)
    spread = jnp.sum(jnp.sum(square, axis=0, keepdims=True), axis=1, keepdims=True)

    def stage_send(stage, triple, peers):
        for j in range(3):
            mom[stage, 0, j:j + 1, :] = jnp.broadcast_to(triple[j], (1, BLK))
        copies = []
        for k, peer in enumerate(peers, 1):
            copy = pltpu.make_async_remote_copy(
                src_ref=mom.at[stage, 0, 0:3], dst_ref=mom.at[stage, k, 0:3],
                send_sem=mom_send.at[stage, k], recv_sem=mom_recv.at[stage, k],
                device_id=peer, device_id_type=MESH)
            copy.start()
            copies.append(copy)
        return copies

    def stage_wait(stage, copies):
        for copy in copies:
            copy.wait_recv()
        return merged(mom[stage])

    pl.semaphore_wait(barrier, 21)
    at_group = stage_send(0, (count, mean, spread), group_peers)

    mate = g + 1 - 2 * lax.rem(g, 2)
    right, left, far = lax.rem(g + 2, 8), lax.rem(g + 6, 8), lax.rem(g + 4, 8)
    low, high, whole = pl.ds(0, HALF), pl.ds(HALF, HALF), pl.ds(0, ROWS)

    def move(i, owner, span, to):
        copy = pltpu.make_async_remote_copy(
            src_ref=gath.at[owner, span], dst_ref=gath.at[owner, span],
            send_sem=data_send.at[i], recv_sem=data_recv.at[i],
            device_id=(d, to), device_id_type=MESH)
        copy.start()
        return copy

    r1 = move(0, g, low, right)
    l1 = move(1, g, high, left)
    r2 = move(2, g, high, right)
    l2 = move(3, g, low, left)
    own = move(4, g, whole, mate)

    to_y = stage_send(1, stage_wait(0, at_group), y_peers)

    r1.wait_recv()
    r3 = move(5, left, low, right)
    l1.wait_recv()
    l3 = move(6, right, high, left)
    m1 = move(7, left, low, mate)
    m2 = move(8, right, high, mate)

    to_z = stage_send(2, stage_wait(1, to_y), z_peers)

    r2.wait_recv()
    m3 = move(9, left, high, mate)
    l2.wait_recv()
    m4 = move(10, right, low, mate)
    r3.wait_recv()
    m5 = move(11, far, low, mate)
    l3.wait_recv()
    m6 = move(12, far, high, mate)
    for copy in (own, m1, m2, m3, m4, m5, m6):
        copy.wait_recv()

    loads[4].wait()

    def gather(i, _):
        for j in range(16):
            slot = i * 16 + j
            want = asg[0, slot]
            row = ((want & 31) << 3) | ((want >> 5) & 7)
            rows[pl.ds(slot, 1), :] = gath[want >> 9, pl.ds((want & 256) + row, 1), :]
        return 0

    lax.fori_loop(0, ROWS // 16, gather, 0)

    n, middle, deviation = stage_wait(2, to_z)
    scale = lax.rsqrt(deviation / n + EPSILON)
    picked = rows[...]
    rows[...] = jnp.where(picked < LIMIT, (picked - middle) * scale, 0.0)
    give_train = pltpu.make_async_copy(rows, train_hbm, out_sem.at[1])
    give_train.start()

    for copy in at_group + to_y + to_z + [r1, l1, r2, l2, own, r3, l3, m1, m2, m3, m4, m5, m6]:
        copy.wait_send()
    give_returns.wait()
    give_train.wait()


def body(rewards, values, horizon, lengths, assignment):
    hbm = pl.BlockSpec(memory_space=pltpu.MemorySpace.HBM)
    f32 = jnp.float32
    return pl.pallas_call(
        kernel,
        out_shape=(jax.ShapeDtypeStruct((SEQ, LEN), f32), jax.ShapeDtypeStruct((ROWS, BLK), f32)),
        in_specs=[hbm] * 5,
        out_specs=(hbm, hbm),
        scratch_shapes=[
            pltpu.VMEM((SEQ, LEN), f32),
            pltpu.VMEM((SEQ, LEN), f32),
            pltpu.VMEM((1, SEQ), f32),
            pltpu.VMEM((1, SEQ), jnp.int32),
            pltpu.SMEM((1, ROWS), jnp.int32),
            pltpu.VMEM((SEQ, LEN), f32),
            pltpu.VMEM((8, ROWS, BLK), f32),
            pltpu.VMEM((ROWS, BLK), f32),
            pltpu.VMEM((3, 8, 8, BLK), f32),
            pltpu.SemaphoreType.DMA((5,)),
            pltpu.SemaphoreType.DMA((2,)),
            pltpu.SemaphoreType.DMA((3, 8)),
            pltpu.SemaphoreType.DMA((3, 8)),
            pltpu.SemaphoreType.DMA((13,)),
            pltpu.SemaphoreType.DMA((13,)),
        ],
        compiler_params=pltpu.CompilerParams(collective_id=0, has_side_effects=True),
        name="advantage",
    )(rewards, values, horizon.reshape(1, SEQ), lengths.reshape(1, SEQ), assignment)


def solution(mesh):
    in_specs = (
        P(("dp", "group"), None),
        P(("dp", "group"), None),
        P(("dp", "group")),
        P(("dp", "group")),
        P("dp", "group"),
    )
    out_specs = (P(("dp", "group"), None), P(("dp", "group"), None))
    return jax.shard_map(body, mesh=mesh, in_specs=in_specs, out_specs=out_specs, check_vma=False)
```

time: 104 us -> 31.5 us (0.30)
  starting transfers between devices: 32.2 us -> 0 us
  Pallas kernels: 0 us -> 28.3 us
  waiting for transfers between devices: 26.4 us -> 0 us
  between operations: 15.1 us -> 0.65 us
  local copies, waits for them, and re-layouts: 15 us -> 2.42 us
  other arithmetic: 7.65 us -> 0 us
  matrix products: 6.89 us -> 0 us
    all_to_all x4 -> x0, starting transfers between devices: 32.2 us -> none  [copy_for_each(): return lax.all_to_all(copies, axis, split_axis=0, concat_axis=0, tiled=True)]
    pallas_call x0 -> x1, Pallas kernels: none -> 28.3 us  [body(): pl.pallas_call(kernel, out_shape=(jax.ShapeDtypeStruct((SEQ, LEN), f32),...]
    all_to_all x4 -> x0, waiting for transfers between devices: 26.4 us -> none  [copy_for_each(): return lax.all_to_all(copies, axis, split_axis=0, concat_axis=0, tiled=True)]
    slice x52 -> x0, local copies, waits for them, and re-layouts: 10.8 us -> none  [the longest x47 7.34 us: combined_pairwise(): part[side::2]]
    dot_general x3 -> x0, matrix products: 6.89 us -> none  [the longest x1 4.48 us: body(): jnp.dot(onehot, flat, precision=lax.Precision.HIGHEST, preferred_element_...]
    broadcast_in_dim x5 -> x0, local copies, waits for them, and re-layouts: 3.52 us -> none  [the longest x4 3.45 us: copy_for_each(): copies = jnp.broadcast_to(shard, (lax.axis_size(axis), *shard.shape))]
    reduce_sum x4 -> x0, other arithmetic: 3.29 us -> none  [the longest x1 1.57 us: body(): counted = jnp.sum(weight)]
    unnamed x7 -> x4, local copies, waits for them, and re-layouts: 0.07 us -> 2.42 us
  transfers between devices with their start and end apart: 4 -> 0, of which waited for: 3 -> 0; matrix products, arithmetic and copies ran while one was open for 11% -> 0% of each run, Pallas kernels for 0% -> 0%
where the time goes in v1:
time: 31.5 us; the launch traced here: 31.3 us
  Pallas kernels  28.3 us (90%)
  local copies, waits for them, and re-layouts  2.42 us (8%)
  between operations  0.65 us (2%)
    pallas_call x1, Pallas kernels, body(): pl.pallas_call(kernel, out_shape=(jax.ShapeDtypeStruct((SEQ, LEN), f32),...  28.3 us
    unnamed x4, local copies, waits for them, and re-layouts  2.42 us

profile of v1, /device:TPU:1, one launch (start us, length us, event | category | flops | bytes accessed | tf_op | source)
XLA Modules:
  0.0 31.3 jit_solution(10717897489032449830)
XLA Ops:
  0.6 28.3 %advantage.1 = (f32[16,4096]{1,0:T(8,128)}, f32[512,128]{1,0:T(8,128)}) custom-call(f32[16,4096]{1,0:T(8,128)} %rew_hbm.1, f32[16,4096]{1,0:T(8,128)} %val_hbm.1, f32[1,16]{1,0:T(1,128)} %bitcast.2, s32[1,16]{1,0:T(1,128)} %bitcast.3, s32[1,512]{1,0:T(1,128)} %asg_hbm.1), custom_call_target="tpu_custom_call" | custom-call | tf_op jit(solution)/shard_map/advantage/pallas_call | solution.py:204
  28.9 0.0 copy-start
  28.9 1.7 %copy.9 = f32[16,4096]{1,0:T(8,128)} copy(f32[16,4096]{1,0:T(8,128)} %get-tuple-element.4) | data formatting | bytes 524288
  30.6 0.0 copy-done
  30.6 0.7 %copy.10 = f32[512,128]{1,0:T(8,128)} copy(f32[512,128]{1,0:T(8,128)S(1)} %copy-done) | data formatting | bytes 524288
Async XLA Ops:
  28.9 1.7 %copy-start = (f32[512,128]{1,0:T(8,128)S(1)}, f32[512,128]{1,0:T(8,128)}, u32[]{:S(2)}) copy-start(f32[512,128]{1,0:T(8,128)} %get-tuple-element.5) | copy-start | bytes 786436

commit v2 on v1

--- a/solution.py
+++ b/solution.py
@@ -27,8 +27,13 @@
     return jnp.broadcast_to(picked, (SEQ, BLK))
 
 
-def merged(buf):
-    n, m, s = buf[:, 0, :], buf[:, 1, :], buf[:, 2, :]
+def as_row(count, mean, spread):
+    lane = lax.broadcasted_iota(jnp.int32, (1, BLK), 1)
+    return jnp.where(lane == 0, count, jnp.where(lane == 1, mean, spread))
+
+
+def merged(rows):
+    n, m, s = (jnp.broadcast_to(rows[:, j:j + 1], rows.shape) for j in range(3))
     total = jnp.sum(n, axis=0, keepdims=True)
     mean = jnp.sum(n * m, axis=0, keepdims=True) / total
     gap = m - mean
@@ -36,19 +41,33 @@
     return total, mean, spread
 
 
-def kernel(rew_hbm, val_hbm, hor_hbm, len_hbm, asg_hbm, ret_hbm, train_hbm,
-           rew, val, hor, lens, asg, ret, gath, rows, mom,
-           in_sem, out_sem, mom_send, mom_recv, data_send, data_recv):
+def each(first, last, act):
+    lax.fori_loop(first, last, lambda k, c: (act(k), c)[1], 0)
+
+
+def kernel(rew_hbm, val_hbm, hor_hbm, len_hbm, asg_hbm, ret, rows, stats,
+           rew, val, hor, lens, asg, gath, plane, line,
+           in_sem, plane_sem, z_sem, here, data_send, data_recv):
     d = lax.axis_index("dp")
     g = lax.axis_index("group")
     y, z = lax.rem(d, 8), d // 8
-    group_peers = [(d, lax.rem(g + k, 8)) for k in range(1, 8)]
-    y_peers = [(z * 8 + lax.rem(y + k, 8), g) for k in range(1, 8)]
-    z_peers = [(lax.rem(d + 8 * k, 64), g) for k in range(1, 8)]
-
-    barrier = pltpu.get_barrier_semaphore()
-    for peer in z_peers + y_peers + group_peers:
-        pl.semaphore_signal(barrier, inc=1, device_id=peer, device_id_type=MESH)
+
+    def signal(sem, where):
+        pl.semaphore_signal(sem, inc=1, device_id=where, device_id_type=MESH)
+
+    def await_signals(sem, count):
+        @pl.when(count > 0)
+        def _():
+            pl.semaphore_wait(sem, count)
+
+    def on_line(k):
+        return k * 8 + y, g
+
+    def on_row(k):
+        return z * 8 + k, g
+
+    def on_plane(k):
+        return z * 8 + k // 8, lax.rem(k, 8)
 
     loads = [
         pltpu.make_async_copy(src, dst, in_sem.at[i])
@@ -57,6 +76,12 @@
     ]
     for load in loads:
         load.start()
+    barrier = pltpu.get_barrier_semaphore()
+    for k in range(1, 8):
+        signal(barrier, (d, lax.rem(g + k, 8)))
+    each(z + 1, 8, lambda k: signal(barrier, on_line(k)))
+    each(y + 1, 8, lambda k: signal(barrier, on_row(k)))
+
     for load in loads[:4]:
         load.wait()
 
@@ -100,8 +125,6 @@
             at = (first + i) * 8
             gath[g, at:at + 8, :] = sent[:8]
             gath[g, HALF + at:HALF + at + 8, :] = sent[8:]
-    give_returns = pltpu.make_async_copy(ret, ret_hbm, out_sem.at[0])
-    give_returns.start()
 
     count = jnp.sum(jnp.sum(length[:, 0:1].astype(jnp.float32), axis=0, keepdims=True), axis=1, keepdims=True)
     mean = jnp.sum(jnp.sum(total, axis=0, keepdims=True), axis=1, keepdims=True) / count
@@ -112,26 +135,20 @@
         square = square + jnp.sum((gap * gap).reshape(8, 8, BLK), axis=0)
     spread = jnp.sum(jnp.sum(square, axis=0, keepdims=True), axis=1, keepdims=True)
 
-    def stage_send(stage, triple, peers):
-        for j in range(3):
-            mom[stage, 0, j:j + 1, :] = jnp.broadcast_to(triple[j], (1, BLK))
-        copies = []
-        for k, peer in enumerate(peers, 1):
-            copy = pltpu.make_async_remote_copy(
-                src_ref=mom.at[stage, 0, 0:3], dst_ref=mom.at[stage, k, 0:3],
-                send_sem=mom_send.at[stage, k], recv_sem=mom_recv.at[stage, k],
-                device_id=peer, device_id_type=MESH)
-            copy.start()
-            copies.append(copy)
-        return copies
-
-    def stage_wait(stage, copies):
-        for copy in copies:
-            copy.wait_recv()
-        return merged(mom[stage])
-
-    pl.semaphore_wait(barrier, 21)
-    at_group = stage_send(0, (count, mean, spread), group_peers)
+    line[pl.ds(z, 1), :] = as_row(count, mean, spread)
+    pl.semaphore_wait(barrier, 7 + z + y)
+
+    def send(buf, slot, sem, to):
+        pltpu.make_async_remote_copy(
+            src_ref=buf.at[pl.ds(slot, 1)], dst_ref=buf.at[pl.ds(slot, 1)],
+            send_sem=sem.at[0], recv_sem=sem.at[1],
+            device_id=to, device_id_type=MESH).start()
+
+    def send_line(k):
+        send(line, z, z_sem, on_line(k))
+
+    each(0, z, send_line)
+    each(0, z, lambda k: signal(here.at[0], on_line(k)))
 
     mate = g + 1 - 2 * lax.rem(g, 2)
     right, left, far = lax.rem(g + 2, 8), lax.rem(g + 6, 8), lax.rem(g + 4, 8)
@@ -151,7 +168,7 @@
     l2 = move(3, g, low, left)
     own = move(4, g, whole, mate)
 
-    to_y = stage_send(1, stage_wait(0, at_group), y_peers)
+    each(0, y, lambda k: signal(here.at[1], on_row(k)))
 
     r1.wait_recv()
     r3 = move(5, left, low, right)
@@ -159,13 +176,22 @@
     l3 = move(6, right, high, left)
     m1 = move(7, left, low, mate)
     m2 = move(8, right, high, mate)
-
-    to_z = stage_send(2, stage_wait(1, to_y), z_peers)
+    await_signals(here.at[1], 7 - y)
+    each(y + 1, 8, lambda k: signal(here.at[2], on_row(k)))
+    await_signals(here.at[0], 7 - z)
+    each(z + 1, 8, send_line)
+    others_z = line.at[pl.ds(0, 7)]
+    pltpu.make_async_copy(others_z, others_z, z_sem.at[1]).wait()
+    mine = y * 8 + g
+    plane[pl.ds(mine, 1), :] = as_row(*merged(line[...]))
+    await_signals(here.at[2], y)
+    each(1, 64, lambda k: send(plane, mine, plane_sem, on_plane(lax.rem(mine + k, 64))))
 
     r2.wait_recv()
     m3 = move(9, left, high, mate)
     l2.wait_recv()
     m4 = move(10, right, low, mate)
+
     r3.wait_recv()
     m5 = move(11, far, low, mate)
     l3.wait_recv()
@@ -185,47 +211,71 @@
 
     lax.fori_loop(0, ROWS // 16, gather, 0)
 
-    n, middle, deviation = stage_wait(2, to_z)
-    scale = lax.rsqrt(deviation / n + EPSILON)
-    picked = rows[...]
-    rows[...] = jnp.where(picked < LIMIT, (picked - middle) * scale, 0.0)
-    give_train = pltpu.make_async_copy(rows, train_hbm, out_sem.at[1])
-    give_train.start()
-
-    for copy in at_group + to_y + to_z + [r1, l1, r2, l2, own, r3, l3, m1, m2, m3, m4, m5, m6]:
+    others = plane.at[pl.ds(0, 63)]
+    pltpu.make_async_copy(others, others, plane_sem.at[1]).wait()
+    n, middle, deviation = merged(plane[...])
+    stats[0:1, :] = middle
+    stats[1:2, :] = lax.rsqrt(deviation / n + EPSILON)
+    pltpu.make_async_copy(others, others, plane_sem.at[0]).wait()
+    pltpu.make_async_copy(others_z, others_z, z_sem.at[0]).wait()
+    for copy in [r1, l1, r2, l2, own, r3, l3, m1, m2, m3, m4, m5, m6]:
         copy.wait_send()
+
+
+def finish(ret, rows, stats, ret_hbm, train_hbm, train, sem):
+    give_returns = pltpu.make_async_copy(ret, ret_hbm, sem.at[0])
+    give_returns.start()
+    middle, scale = stats[0:1, :], stats[1:2, :]
+    gives = []
+    for i in range(2):
+        part = slice(i * HALF, (i + 1) * HALF)
+        picked = rows[part, :]
+        train[part, :] = jnp.where(picked < LIMIT, (picked - middle) * scale, 0.0)
+        give = pltpu.make_async_copy(train.at[part], train_hbm.at[part], sem.at[1 + i])
+        give.start()
+        gives.append(give)
     give_returns.wait()
-    give_train.wait()
+    for give in gives:
+        give.wait()
 
 
 def body(rewards, values, horizon, lengths, assignment):
     hbm = pl.BlockSpec(memory_space=pltpu.MemorySpace.HBM)
     f32 = jnp.float32
-    return pl.pallas_call(
+    vmem = pl.BlockSpec(memory_space=pltpu.MemorySpace.VMEM)
+    ret, rows, stats = pl.pallas_call(
         kernel,
-        out_shape=(jax.ShapeDtypeStruct((SEQ, LEN), f32), jax.ShapeDtypeStruct((ROWS, BLK), f32)),
+        out_shape=tuple(jax.ShapeDtypeStruct(shape, f32) for shape in ((SEQ, LEN), (ROWS, BLK), (8, BLK))),
         in_specs=[hbm] * 5,
-        out_specs=(hbm, hbm),
+        out_specs=(vmem, vmem, vmem),
         scratch_shapes=[
             pltpu.VMEM((SEQ, LEN), f32),
             pltpu.VMEM((SEQ, LEN), f32),
             pltpu.VMEM((1, SEQ), f32),
             pltpu.VMEM((1, SEQ), jnp.int32),
             pltpu.SMEM((1, ROWS), jnp.int32),
-            pltpu.VMEM((SEQ, LEN), f32),
             pltpu.VMEM((8, ROWS, BLK), f32),
-            pltpu.VMEM((ROWS, BLK), f32),
-            pltpu.VMEM((3, 8, 8, BLK), f32),
+            pltpu.VMEM((64, BLK), f32),
+            pltpu.VMEM((8, BLK), f32),
             pltpu.SemaphoreType.DMA((5,)),
             pltpu.SemaphoreType.DMA((2,)),
-            pltpu.SemaphoreType.DMA((3, 8)),
-            pltpu.SemaphoreType.DMA((3, 8)),
+            pltpu.SemaphoreType.DMA((2,)),
+            pltpu.SemaphoreType.REGULAR((3,)),
             pltpu.SemaphoreType.DMA((13,)),
             pltpu.SemaphoreType.DMA((13,)),
         ],
-        compiler_params=pltpu.CompilerParams(collective_id=0, has_side_effects=True),
+        compiler_params=pltpu.CompilerParams(collective_id=0, has_side_effects=True, vmem_limit_bytes=16 << 20),
         name="advantage",
-    )(rewards, values, horizon.reshape(1, SEQ), lengths.reshape(1, SEQ), assignment)
+    )(*(pltpu.with_memory_space_constraint(x, pltpu.MemorySpace.HBM) for x in (rewards, values, horizon.reshape(1, SEQ), lengths.reshape(1, SEQ), assignment)))
+    return pl.pallas_call(
+        finish,
+        out_shape=(jax.ShapeDtypeStruct((SEQ, LEN), f32), jax.ShapeDtypeStruct((ROWS, BLK), f32)),
+        in_specs=[vmem] * 3,
+        out_specs=(hbm, hbm),
+        scratch_shapes=[pltpu.VMEM((ROWS, BLK), f32), pltpu.SemaphoreType.DMA((3,))],
+        compiler_params=pltpu.CompilerParams(vmem_limit_bytes=4 << 20),
+        name="finish",
+    )(ret, rows, stats)
 
 
 def solution(mesh):

time: 31.5 us -> 26.7 us (0.85)
  local copies, waits for them, and re-layouts: 2.42 us -> 0 us
  Pallas kernels: 28.3 us -> 26 us
    unnamed x4 -> x0, local copies, waits for them, and re-layouts: 2.42 us -> none
    pallas_call x1 -> x2, Pallas kernels: 28.3 us -> 26 us  [the longest x1 25.1 us: body(): pl.pallas_call(kernel, out_shape=tuple((jax.ShapeDtypeStruct(shape, f32)...]
where the time goes in v2:
time: 26.7 us; the launch traced here: 26.6 us
  Pallas kernels  26 us (97%)
  between operations  0.64 us (2%)
    pallas_call x1, Pallas kernels, body(): pl.pallas_call(kernel, out_shape=tuple((jax.ShapeDtypeStruct(shape, f32)...  25.1 us
    pallas_call x1, Pallas kernels, body(): pl.pallas_call(finish, out_shape=(jax.ShapeDtypeStruct((SEQ, LEN), f32),...  0.81 us

profile of v2, /device:TPU:1, one launch (start us, length us, event | category | flops | bytes accessed | tf_op | source)
XLA Modules:
  0.0 26.6 jit_solution(16037595320873255906)
XLA Ops:
  0.6 25.1 %advantage.1 = (f32[16,4096]{1,0:T(8,128)S(1)}, f32[512,128]{1,0:T(8,128)S(1)}, f32[8,128]{1,0:T(8,128)S(1)}) custom-call(f32[16,4096]{1,0:T(8,128)} %rew_hbm.1, f32[16,4096]{1,0:T(8,128)} %val_hbm.1, f32[1,16]{1,0:T(1,128)} %bitcast.2, s32[1,16]{1,0:T(1,128)} %bitcast.3, s32[1,512]{1,0:T(1,128)} %asg_hbm.1), custom_call_target="tpu_custom_call" | custom-call | tf_op jit(solution)/shard_map/advantage/pallas_call | solution.py:246
  25.8 0.8 %finish.1 = (f32[16,4096]{1,0:T(8,128)}, f32[512,128]{1,0:T(8,128)}) custom-call(f32[16,4096]{1,0:T(8,128)S(1)} %get-tuple-element.5.ret, f32[512,128]{1,0:T(8,128)S(1)} %get-tuple-element.6.rows, f32[8,128]{1,0:T(8,128)S(1)} %get-tuple-element.7.stats), custom_call_target="tpu_custom_call" | custom-call | tf_op jit(solution)/shard_map/finish/pallas_call | solution.py:270

commit v3 on v2

--- a/solution.py
+++ b/solution.py
@@ -12,6 +12,7 @@
 ROWS = SEQ * NBLK
 HALF = ROWS // 2
 TRACE_DECAY = 0.998
+MORE = 1.0 / TRACE_DECAY - 1.0
 EPSILON = 1e-05
 OUTSIDE = 1e30
 LIMIT = 1e29
@@ -76,51 +77,54 @@
     ]
     for load in loads:
         load.start()
+
     barrier = pltpu.get_barrier_semaphore()
     for k in range(1, 8):
         signal(barrier, (d, lax.rem(g + k, 8)))
     each(z + 1, 8, lambda k: signal(barrier, on_line(k)))
     each(y + 1, 8, lambda k: signal(barrier, on_row(k)))
 
-    for load in loads[:4]:
-        load.wait()
+    loads[0].wait()
+    loads[1].wait()
 
     lane = lax.broadcasted_iota(jnp.int32, (SEQ, BLK), 1)
     length = column(lens[...].astype(jnp.float32)).astype(jnp.int32)
     gamma = 1.0 - 1.0 / column(hor[...])
-    powers = [gamma * TRACE_DECAY]
-    for _ in range(7):
-        powers.append(powers[-1] * powers[-1])
-    steps = [jnp.where(lane < BLK - (1 << k), powers[k], 0.0) for k in range(7)]
-    togo = BLK - lane
-    tail = jnp.where(togo == BLK, powers[7], 1.0)
+    power = gamma * TRACE_DECAY
+    rise = jnp.ones((SEQ, BLK), jnp.float32)
     for k in range(7):
-        tail = tail * jnp.where(((togo >> k) & 1) == 1, powers[k], 1.0)
-
+        rise = rise * jnp.where(((lane >> k) & 1) == 1, power, 1.0)
+        power = power * power
+    fall = 1.0 / rise
+    down = lax.broadcasted_iota(jnp.int32, (BLK, 2 * BLK), 0)
+    across = lax.broadcasted_iota(jnp.int32, (BLK, 2 * BLK), 1)
+    ones = jnp.where((across >= BLK) | (down >= across), 1.0, 0.0).astype(jnp.bfloat16)
+    twice = jnp.concatenate([ones, ones], axis=0)
+    past = lane - length
     zero = jnp.zeros((SEQ, BLK), jnp.float32)
-    carry, ahead, total = zero, zero, zero
+    carry, total = zero, zero
     shape = (CHUNK, SEQ, BLK)
+    loads[2].wait()
+    loads[3].wait()
     for first in range(NBLK - CHUNK, -1, -CHUNK):
         cols = [slice((first + i) * BLK, (first + i + 1) * BLK) for i in range(CHUNK)]
         v = jnp.stack([val[:, c] for c in cols])
         r = jnp.stack([rew[:, c] for c in cols])
-        turned = pltpu.roll(v, BLK - 1, 2)
-        following = jnp.concatenate([turned[1:], ahead[None]], axis=0)
-        ahead = turned[0]
-        shifted = jnp.where(lane[None] < BLK - 1, turned, following)
-        block = lax.broadcasted_iota(jnp.int32, shape, 0) + first
-        left = length[None] - block * BLK
-        inside = lane[None] < left
-        follows = lane[None] + 1 < left
-        part = jnp.where(inside, r + gamma[None] * jnp.where(follows, shifted, 0.0) - v, 0.0)
-        for k in range(7):
-            part = part + steps[k][None] * pltpu.roll(part, BLK - (1 << k), 2)
-        head = jnp.broadcast_to(part[:, :, 0:1], shape)
+        inside = jnp.stack([past < -(first + i) * BLK for i in range(CHUNK)])
+        part = jnp.where(inside, r + MORE * v, 0.0)
+        scaled = (part * rise[None]).reshape(CHUNK * SEQ, BLK)
+        high = scaled.astype(jnp.bfloat16)
+        rest = scaled - high.astype(jnp.float32)
+        middle = rest.astype(jnp.bfloat16)
+        low = (rest - middle.astype(jnp.float32)).astype(jnp.bfloat16)
+        sums = jnp.dot(jnp.concatenate([high, middle], axis=1), twice, preferred_element_type=jnp.float32)
+        sums = sums + jnp.dot(low, ones, preferred_element_type=jnp.float32)
+        inner, whole_block = sums[:, :BLK].reshape(shape), sums[:, BLK:].reshape(shape)
         for i in range(CHUNK - 1, -1, -1):
-            adv = part[i] + tail * carry
-            carry = head[i] + powers[7] * carry
-            total = total + adv
-            ret[:, cols[i]] = jnp.where(inside[i], adv + v[i], 0.0)
+            tail = power * carry
+            adv = (inner[i] + tail) * fall - (1.0 + MORE) * v[i]
+            carry = whole_block[i] + tail
+            total = total + jnp.where(inside[i], adv, 0.0)
             sent = jnp.where(inside[i], adv, OUTSIDE)
             at = (first + i) * 8
             gath[g, at:at + 8, :] = sent[:8]
@@ -169,6 +173,13 @@
     own = move(4, g, whole, mate)
 
     each(0, y, lambda k: signal(here.at[1], on_row(k)))
+
+    for i in range(NBLK):
+        col = slice(i * BLK, (i + 1) * BLK)
+        for h in range(2):
+            seqs = slice(h * 8, h * 8 + 8)
+            adv = gath[g, h * HALF + i * 8:h * HALF + i * 8 + 8, :]
+            ret[seqs, col] = jnp.where(adv < LIMIT, adv + val[seqs, col], 0.0)
 
     r1.wait_recv()
     r3 = move(5, left, low, right)
@@ -185,7 +196,11 @@
     mine = y * 8 + g
     plane[pl.ds(mine, 1), :] = as_row(*merged(line[...]))
     await_signals(here.at[2], y)
-    each(1, 64, lambda k: send(plane, mine, plane_sem, on_plane(lax.rem(mine + k, 64))))
+    def send_plane(k):
+        send(plane, mine, plane_sem, on_plane(k))
+
+    each(0, mine, send_plane)
+    each(mine + 1, 64, send_plane)
 
     r2.wait_recv()
     m3 = move(9, left, high, mate)

time: 26.7 us -> 25.7 us (0.963)
  Pallas kernels: 26 us -> 24.9 us
    pallas_call x1, Pallas kernels: 25.1 us -> 24.1 us  [body(): pl.pallas_call(kernel, out_shape=tuple((jax.ShapeDtypeStruct(shape, f32)...]
where the time goes in v3:
time: 25.7 us; the launch traced here: 25.6 us
  Pallas kernels  24.9 us (97%)
  between operations  0.64 us (2%)
    pallas_call x1, Pallas kernels, body(): pl.pallas_call(kernel, out_shape=tuple((jax.ShapeDtypeStruct(shape, f32)...  24.1 us
    pallas_call x1, Pallas kernels, body(): pl.pallas_call(finish, out_shape=(jax.ShapeDtypeStruct((SEQ, LEN), f32),...  0.81 us

profile of v3, /device:TPU:1, one launch (start us, length us, event | category | flops | bytes accessed | tf_op | source)
XLA Modules:
  0.0 25.6 jit_solution(6540029479342179340)
XLA Ops:
  0.6 24.1 %advantage.1 = (f32[16,4096]{1,0:T(8,128)S(1)}, f32[512,128]{1,0:T(8,128)S(1)}, f32[8,128]{1,0:T(8,128)S(1)}) custom-call(f32[16,4096]{1,0:T(8,128)} %rew_hbm.1, f32[16,4096]{1,0:T(8,128)} %val_hbm.1, f32[1,16]{1,0:T(1,128)} %bitcast.2, s32[1,16]{1,0:T(1,128)} %bitcast.3, s32[1,512]{1,0:T(1,128)} %asg_hbm.1), custom_call_target="tpu_custom_call" | custom-call | tf_op jit(solution)/shard_map/advantage/pallas_call | solution.py:261
  24.7 0.8 %finish.1 = (f32[16,4096]{1,0:T(8,128)}, f32[512,128]{1,0:T(8,128)}) custom-call(f32[16,4096]{1,0:T(8,128)S(1)} %get-tuple-element.5.ret, f32[512,128]{1,0:T(8,128)S(1)} %get-tuple-element.6.rows, f32[8,128]{1,0:T(8,128)S(1)} %get-tuple-element.7.stats), custom_call_target="tpu_custom_call" | custom-call | tf_op jit(solution)/shard_map/finish/pallas_call | solution.py:285

commit v4 on v3

--- a/solution.py
+++ b/solution.py
@@ -47,8 +47,8 @@
 
 
 def kernel(rew_hbm, val_hbm, hor_hbm, len_hbm, asg_hbm, ret, rows, stats,
-           rew, val, hor, lens, asg, gath, plane, line,
-           in_sem, plane_sem, z_sem, here, data_send, data_recv):
+           rew, val, hor, lens, wants, asg, gath, plane, line,
+           in_sem, plane_sem, z_sem, here, above, data_send, data_recv):
     d = lax.axis_index("dp")
     g = lax.axis_index("group")
     y, z = lax.rem(d, 8), d // 8
@@ -73,16 +73,16 @@
     loads = [
         pltpu.make_async_copy(src, dst, in_sem.at[i])
         for i, (src, dst) in enumerate(
-            [(hor_hbm, hor), (len_hbm, lens), (val_hbm, val), (rew_hbm, rew), (asg_hbm, asg)])
+            [(hor_hbm, hor), (len_hbm, lens), (val_hbm, val), (rew_hbm, rew), (asg_hbm, wants)])
     ]
     for load in loads:
         load.start()
 
     barrier = pltpu.get_barrier_semaphore()
-    for k in range(1, 8):
+    each(z + 1, 8, lambda k: signal(barrier, on_line(z + 8 - k)))
+    each(y + 1, 8, lambda k: signal(barrier, on_row(y + 8 - k)))
+    for k in (4, 3, 5, 2, 6, 1, 7):
         signal(barrier, (d, lax.rem(g + k, 8)))
-    each(z + 1, 8, lambda k: signal(barrier, on_line(k)))
-    each(y + 1, 8, lambda k: signal(barrier, on_row(k)))
 
     loads[0].wait()
     loads[1].wait()
@@ -152,7 +152,7 @@
         send(line, z, z_sem, on_line(k))
 
     each(0, z, send_line)
-    each(0, z, lambda k: signal(here.at[0], on_line(k)))
+    each(0, z, lambda k: signal(above.at[z], on_line(k)))
 
     mate = g + 1 - 2 * lax.rem(g, 2)
     right, left, far = lax.rem(g + 2, 8), lax.rem(g + 6, 8), lax.rem(g + 4, 8)
@@ -172,7 +172,11 @@
     l2 = move(3, g, low, left)
     own = move(4, g, whole, mate)
 
-    each(0, y, lambda k: signal(here.at[1], on_row(k)))
+    each(0, y, lambda k: signal(here.at[0], on_row(k)))
+
+    loads[4].wait()
+    want = wants[...]
+    wants[...] = (want - lax.rem(want, 256)) + lax.rem(want, 32) * 8 + lax.rem(want // 32, 8)
 
     for i in range(NBLK):
         col = slice(i * BLK, (i + 1) * BLK)
@@ -181,26 +185,36 @@
             adv = gath[g, h * HALF + i * 8:h * HALF + i * 8 + 8, :]
             ret[seqs, col] = jnp.where(adv < LIMIT, adv + val[seqs, col], 0.0)
 
+    number = pltpu.make_async_copy(wants, asg, in_sem.at[5])
+    number.start()
+
     r1.wait_recv()
     r3 = move(5, left, low, right)
     l1.wait_recv()
     l3 = move(6, right, high, left)
     m1 = move(7, left, low, mate)
     m2 = move(8, right, high, mate)
-    await_signals(here.at[1], 7 - y)
-    each(y + 1, 8, lambda k: signal(here.at[2], on_row(k)))
-    await_signals(here.at[0], 7 - z)
-    each(z + 1, 8, send_line)
+    await_signals(here.at[0], 7 - y)
+    each(y + 1, 8, lambda k: signal(here.at[1], on_row(k)))
+
+    def send_up(k):
+        pl.semaphore_wait(above.at[k], 1)
+        send_line(k)
+
+    each(z + 1, 8, send_up)
     others_z = line.at[pl.ds(0, 7)]
     pltpu.make_async_copy(others_z, others_z, z_sem.at[1]).wait()
     mine = y * 8 + g
     plane[pl.ds(mine, 1), :] = as_row(*merged(line[...]))
-    await_signals(here.at[2], y)
+    await_signals(here.at[1], y)
+
     def send_plane(k):
         send(plane, mine, plane_sem, on_plane(k))
 
-    each(0, mine, send_plane)
-    each(mine + 1, 64, send_plane)
+    for k in range(8):
+        pl.when(mine != k)(lambda k=k: send_plane(k))
+    each(8, mine, send_plane)
+    each(lax.max(mine + 1, 8), 64, send_plane)
 
     r2.wait_recv()
     m3 = move(9, left, high, mate)
@@ -214,14 +228,14 @@
     for copy in (own, m1, m2, m3, m4, m5, m6):
         copy.wait_recv()
 
-    loads[4].wait()
+    number.wait()
+
+    flat = gath.reshape(8 * ROWS, BLK)
 
     def gather(i, _):
         for j in range(16):
             slot = i * 16 + j
-            want = asg[0, slot]
-            row = ((want & 31) << 3) | ((want >> 5) & 7)
-            rows[pl.ds(slot, 1), :] = gath[want >> 9, pl.ds((want & 256) + row, 1), :]
+            rows[pl.ds(slot, 1), :] = flat[pl.ds(asg[0, slot], 1), :]
         return 0
 
     lax.fori_loop(0, ROWS // 16, gather, 0)
@@ -268,14 +282,16 @@
             pltpu.VMEM((SEQ, LEN), f32),
             pltpu.VMEM((1, SEQ), f32),
             pltpu.VMEM((1, SEQ), jnp.int32),
+            pltpu.VMEM((1, ROWS), jnp.int32),
             pltpu.SMEM((1, ROWS), jnp.int32),
             pltpu.VMEM((8, ROWS, BLK), f32),
             pltpu.VMEM((64, BLK), f32),
             pltpu.VMEM((8, BLK), f32),
-            pltpu.SemaphoreType.DMA((5,)),
+            pltpu.SemaphoreType.DMA((6,)),
             pltpu.SemaphoreType.DMA((2,)),
             pltpu.SemaphoreType.DMA((2,)),
-            pltpu.SemaphoreType.REGULAR((3,)),
+            pltpu.SemaphoreType.REGULAR((2,)),
+            pltpu.SemaphoreType.REGULAR((8,)),
             pltpu.SemaphoreType.DMA((13,)),
             pltpu.SemaphoreType.DMA((13,)),
         ],

time: 25.7 us -> 25.8 us (level)
  no operation moved by 1% of the time
where the time goes in v4:
time: 25.8 us; the launch traced here: 25.6 us
  Pallas kernels  25 us (97%)
  between operations  0.64 us (2%)
    pallas_call x1, Pallas kernels, body(): pl.pallas_call(kernel, out_shape=tuple((jax.ShapeDtypeStruct(shape, f32)...  24.2 us
    pallas_call x1, Pallas kernels, body(): pl.pallas_call(finish, out_shape=(jax.ShapeDtypeStruct((SEQ, LEN), f32),...  0.81 us

profile of v4, /device:TPU:1, one launch (start us, length us, event | category | flops | bytes accessed | tf_op | source)
XLA Modules:
  0.0 25.6 jit_solution(6035435990583877874)
XLA Ops:
  0.6 24.2 %advantage.1 = (f32[16,4096]{1,0:T(8,128)S(1)}, f32[512,128]{1,0:T(8,128)S(1)}, f32[8,128]{1,0:T(8,128)S(1)}) custom-call(f32[16,4096]{1,0:T(8,128)} %rew_hbm.1, f32[16,4096]{1,0:T(8,128)} %val_hbm.1, f32[1,16]{1,0:T(1,128)} %bitcast.2, s32[1,16]{1,0:T(1,128)} %bitcast.3, s32[1,512]{1,0:T(1,128)} %asg_hbm.1), custom_call_target="tpu_custom_call" | custom-call | tf_op jit(solution)/shard_map/advantage/pallas_call | solution.py:275
  24.8 0.8 %finish.1 = (f32[16,4096]{1,0:T(8,128)}, f32[512,128]{1,0:T(8,128)}) custom-call(f32[16,4096]{1,0:T(8,128)S(1)} %get-tuple-element.5.ret, f32[512,128]{1,0:T(8,128)S(1)} %get-tuple-element.6.rows, f32[8,128]{1,0:T(8,128)S(1)} %get-tuple-element.7.stats), custom_call_target="tpu_custom_call" | custom-call | tf_op jit(solution)/shard_map/finish/pallas_call | solution.py:301

commit v5 on v4

--- a/solution.py
+++ b/solution.py
@@ -61,14 +61,16 @@
         def _():
             pl.semaphore_wait(sem, count)
 
+    core = lax.rem(g, 2)
+
     def on_line(k):
-        return k * 8 + y, g
+        return k // 2 * 8 + y, g - core + lax.rem(k, 2)
 
     def on_row(k):
         return z * 8 + k, g
 
     def on_plane(k):
-        return z * 8 + k // 8, lax.rem(k, 8)
+        return z * 8 + k // 4, lax.rem(k, 4) * 2 + core
 
     loads = [
         pltpu.make_async_copy(src, dst, in_sem.at[i])
@@ -79,7 +81,7 @@
         load.start()
 
     barrier = pltpu.get_barrier_semaphore()
-    each(z + 1, 8, lambda k: signal(barrier, on_line(z + 8 - k)))
+    each(2 * z + 2, 16, lambda k: signal(barrier, on_line(2 * z + 17 - k)))
     each(y + 1, 8, lambda k: signal(barrier, on_row(y + 8 - k)))
     for k in (4, 3, 5, 2, 6, 1, 7):
         signal(barrier, (d, lax.rem(g + k, 8)))
@@ -139,8 +141,9 @@
         square = square + jnp.sum((gap * gap).reshape(8, 8, BLK), axis=0)
     spread = jnp.sum(jnp.sum(square, axis=0, keepdims=True), axis=1, keepdims=True)
 
-    line[pl.ds(z, 1), :] = as_row(count, mean, spread)
-    pl.semaphore_wait(barrier, 7 + z + y)
+    spot = 2 * z + core
+    line[pl.ds(spot, 1), :] = as_row(count, mean, spread)
+    pl.semaphore_wait(barrier, 7 + 2 * z + y)
 
     def send(buf, slot, sem, to):
         pltpu.make_async_remote_copy(
@@ -149,10 +152,11 @@
             device_id=to, device_id_type=MESH).start()
 
     def send_line(k):
-        send(line, z, z_sem, on_line(k))
-
-    each(0, z, send_line)
-    each(0, z, lambda k: signal(above.at[z], on_line(k)))
+        send(line, spot, z_sem, on_line(k))
+
+    each(0, 2 * z, send_line)
+    send_line(spot + 1 - 2 * core)
+    each(0, 2 * z, lambda k: signal(above.at[spot], on_line(k)))
 
     mate = g + 1 - 2 * lax.rem(g, 2)
     right, left, far = lax.rem(g + 2, 8), lax.rem(g + 6, 8), lax.rem(g + 4, 8)
@@ -201,20 +205,20 @@
         pl.semaphore_wait(above.at[k], 1)
         send_line(k)
 
-    each(z + 1, 8, send_up)
-    others_z = line.at[pl.ds(0, 7)]
+    each(2 * z + 2, 16, send_up)
+    others_z = line.at[pl.ds(0, 15)]
     pltpu.make_async_copy(others_z, others_z, z_sem.at[1]).wait()
-    mine = y * 8 + g
+    mine = y * 4 + g // 2
     plane[pl.ds(mine, 1), :] = as_row(*merged(line[...]))
     await_signals(here.at[1], y)
 
     def send_plane(k):
         send(plane, mine, plane_sem, on_plane(k))
 
-    for k in range(8):
+    for k in range(4):
         pl.when(mine != k)(lambda k=k: send_plane(k))
-    each(8, mine, send_plane)
-    each(lax.max(mine + 1, 8), 64, send_plane)
+    each(4, mine, send_plane)
+    each(lax.max(mine + 1, 4), 32, send_plane)
 
     r2.wait_recv()
     m3 = move(9, left, high, mate)
@@ -240,7 +244,7 @@
 
     lax.fori_loop(0, ROWS // 16, gather, 0)
 
-    others = plane.at[pl.ds(0, 63)]
+    others = plane.at[pl.ds(0, 31)]
     pltpu.make_async_copy(others, others, plane_sem.at[1]).wait()
     n, middle, deviation = merged(plane[...])
     stats[0:1, :] = middle
@@ -285,13 +289,13 @@
             pltpu.VMEM((1, ROWS), jnp.int32),
             pltpu.SMEM((1, ROWS), jnp.int32),
             pltpu.VMEM((8, ROWS, BLK), f32),
-            pltpu.VMEM((64, BLK), f32),
-            pltpu.VMEM((8, BLK), f32),
+            pltpu.VMEM((32, BLK), f32),
+            pltpu.VMEM((16, BLK), f32),
             pltpu.SemaphoreType.DMA((6,)),
             pltpu.SemaphoreType.DMA((2,)),
             pltpu.SemaphoreType.DMA((2,)),
             pltpu.SemaphoreType.REGULAR((2,)),
-            pltpu.SemaphoreType.REGULAR((8,)),
+            pltpu.SemaphoreType.REGULAR((16,)),
             pltpu.SemaphoreType.DMA((13,)),
             pltpu.SemaphoreType.DMA((13,)),
         ],

time: 25.8 us -> 25 us (0.969)
  Pallas kernels: 25 us -> 24.2 us
    pallas_call x1, Pallas kernels: 24.2 us -> 23.4 us  [body(): pl.pallas_call(kernel, out_shape=tuple((jax.ShapeDtypeStruct(shape, f32)...]
where the time goes in v5:
time: 25 us; the launch traced here: 24.9 us
  Pallas kernels  24.2 us (97%)
  between operations  0.64 us (3%)
    pallas_call x1, Pallas kernels, body(): pl.pallas_call(kernel, out_shape=tuple((jax.ShapeDtypeStruct(shape, f32)...  23.4 us
    pallas_call x1, Pallas kernels, body(): pl.pallas_call(finish, out_shape=(jax.ShapeDtypeStruct((SEQ, LEN), f32),...  0.81 us

profile of v5, /device:TPU:1, one launch (start us, length us, event | category | flops | bytes accessed | tf_op | source)
XLA Modules:
  0.0 24.9 jit_solution(9372878349509429525)
XLA Ops:
  0.6 23.4 %advantage.1 = (f32[16,4096]{1,0:T(8,128)S(1)}, f32[512,128]{1,0:T(8,128)S(1)}, f32[8,128]{1,0:T(8,128)S(1)}) custom-call(f32[16,4096]{1,0:T(8,128)} %rew_hbm.1, f32[16,4096]{1,0:T(8,128)} %val_hbm.1, f32[1,16]{1,0:T(1,128)} %bitcast.2, s32[1,16]{1,0:T(1,128)} %bitcast.3, s32[1,512]{1,0:T(1,128)} %asg_hbm.1), custom_call_target="tpu_custom_call" | custom-call | tf_op jit(solution)/shard_map/advantage/pallas_call | solution.py:279
  24.1 0.8 %finish.1 = (f32[16,4096]{1,0:T(8,128)}, f32[512,128]{1,0:T(8,128)}) custom-call(f32[16,4096]{1,0:T(8,128)S(1)} %get-tuple-element.5.ret, f32[512,128]{1,0:T(8,128)S(1)} %get-tuple-element.6.rows, f32[8,128]{1,0:T(8,128)S(1)} %get-tuple-element.7.stats), custom_call_target="tpu_custom_call" | custom-call | tf_op jit(solution)/shard_map/finish/pallas_call | solution.py:305

commit v6 on v5

--- a/solution.py
+++ b/solution.py
@@ -215,10 +215,8 @@
     def send_plane(k):
         send(plane, mine, plane_sem, on_plane(k))
 
-    for k in range(4):
+    for k in range(32):
         pl.when(mine != k)(lambda k=k: send_plane(k))
-    each(4, mine, send_plane)
-    each(lax.max(mine + 1, 4), 32, send_plane)
 
     r2.wait_recv()
     m3 = move(9, left, high, mate)

time: 25 us -> 25 us (level)
  no operation moved by 1% of the time
where the time goes in v6:
time: 25 us; the launch traced here: 24.9 us
  Pallas kernels  24.2 us (97%)
  between operations  0.64 us (3%)
    pallas_call x1, Pallas kernels, body(): pl.pallas_call(kernel, out_shape=tuple((jax.ShapeDtypeStruct(shape, f32)...  23.4 us
    pallas_call x1, Pallas kernels, body(): pl.pallas_call(finish, out_shape=(jax.ShapeDtypeStruct((SEQ, LEN), f32),...  0.81 us

profile of v6, /device:TPU:1, one launch (start us, length us, event | category | flops | bytes accessed | tf_op | source)
XLA Modules:
  0.0 24.9 jit_solution(93577605363125134)
XLA Ops:
  0.6 23.4 %advantage.1 = (f32[16,4096]{1,0:T(8,128)S(1)}, f32[512,128]{1,0:T(8,128)S(1)}, f32[8,128]{1,0:T(8,128)S(1)}) custom-call(f32[16,4096]{1,0:T(8,128)} %rew_hbm.1, f32[16,4096]{1,0:T(8,128)} %val_hbm.1, f32[1,16]{1,0:T(1,128)} %bitcast.2, s32[1,16]{1,0:T(1,128)} %bitcast.3, s32[1,512]{1,0:T(1,128)} %asg_hbm.1), custom_call_target="tpu_custom_call" | custom-call | tf_op jit(solution)/shard_map/advantage/pallas_call | solution.py:277
  24.0 0.8 %finish.1 = (f32[16,4096]{1,0:T(8,128)}, f32[512,128]{1,0:T(8,128)}) custom-call(f32[16,4096]{1,0:T(8,128)S(1)} %get-tuple-element.5.ret, f32[512,128]{1,0:T(8,128)S(1)} %get-tuple-element.6.rows, f32[8,128]{1,0:T(8,128)S(1)} %get-tuple-element.7.stats), custom_call_target="tpu_custom_call" | custom-call | tf_op jit(solution)/shard_map/finish/pallas_call | solution.py:303
